TPU v7x, 512 devices: a whole 4x4x16 slice. The times are simulated.
512 devices in a mesh: sa: 16 (over z_lo, core), sb: 16 (over y, x), noise: 2 (over z_hi).
Axes of the slice: x: 4, y: 4, z: 16 (z_hi: 2, z_lo: 8; z = z_hi * 8 + z_lo), core: 2. Of those that a mesh axis runs over, the one named last changes fastest.
Arguments:
- base: bfloat16 [8192, 1536], P(('sa', 'sb')), may hold values from -6 to 6
- noise: bfloat16 [4, 8192, 1536], P('noise', ('sa', 'sb')), may hold values from -3 to 3
- cot: bfloat16 [8192, 1536], P(('sa', 'sb')), may hold values from -6 to 6
- convolution_weight: bfloat16 [3, 1536, 384], P(None, 'sa'), may hold values from -0.15625 to 0.15625
- mix_w: bfloat16 [384, 1536], P('sa'), may hold values from -0.625 to 0.625
- norm_gain: float32 [1536], replicated, may hold values from 0.1 to 1.9
- qkv_w: bfloat16 [1536, 896], P('sa'), may hold values from -1 to 1
- out_w: bfloat16 [384, 1536], P('sa'), may hold values from -1.25 to 1.25
- band_width: int32 [4], replicated, may hold values from 1 to 32, as said below
- pairs: int32 [64, 2], replicated, may hold values from 0 to 63, as said below
Outputs:
- saliency: float32 [8192, 1536], P(('sa', 'sb'))
Inputs may be any that keep to these rules, and one draw needn't show every extreme that they name: `band_width`: one head has band half-width exactly 32. Tile t holds bins t * 128 to (t + 1) * 128 - 1; both tiles of a pair lie in the same stretch of 512 bins that starts at a multiple of 512; pairs may repeat.
All inputs are finite; a program needn't handle non-finite values.
Results may differ from a plain program's by a relative error of at most 0.018.
Values may be sent and summed in bfloat16 or wider, within the bound.
A program may use at most 64 MiB of HBM per device.

v0:
```python
import jax
import jax.numpy as jnp
from jax import lax
from jax.sharding import PartitionSpec as P

HID = 384
HEADS = 4
KEY = 64
VAL = 96
DILATION_BINS = 16
BAND = 32
TILE = 128
ROOT_TWO_PI = 0.7978845608
CUBIC = 0.044715


def extended(value, sides, width):
    for axis, dim in sides:
        peers, length = (lax.axis_size(axis), value.shape[dim])
        up = [(i, (i + 1) % peers) for i in range(peers - 1)]
        down = [(j, i) for i, j in up]
        last = lax.slice_in_dim(value, length - width, length, axis=dim)
        leading = lax.slice_in_dim(value, 0, width, axis=dim)
        before = lax.ppermute(last, axis, up)
        after = lax.ppermute(leading, axis, down)
        value = jnp.concatenate([before, value, after], axis=dim)
    return value


def from_behind(block, axis, distance):
    devices = range(lax.axis_size(axis))
    route = [(i - distance, i) for i in devices if i - distance in devices]
    return lax.ppermute(block, axis, route)


def gelu_tanh(values):
    inner = ROOT_TWO_PI * (values + CUBIC * values * values * values)
    return 0.5 * values * (1.0 + jnp.tanh(inner))


def gelu_slope(values):
    tangent = jnp.tanh(ROOT_TWO_PI * (values + CUBIC * values * values * values))
    return 0.5 * (1.0 + tangent) + 0.5 * values * (1.0 - tangent * tangent) * ROOT_TWO_PI * (
        1.0 + 3.0 * CUBIC * values * values
    )


def shards(base, noise, cot, convolution_weight, mix_w, norm_gain, qkv_w, out_w, band_width, pairs):
    conv_full, mix_full, qkv_full, out_full = (
        lax.all_gather(convolution_weight, "sa", axis=1, tiled=True),
        lax.all_gather(mix_w, "sa", axis=0, tiled=True),
        lax.all_gather(qkv_w, "sa", axis=0, tiled=True),
        lax.all_gather(out_w, "sa", axis=0, tiled=True),
    )
    sequence_bins = base.shape[0]
    samples_dev = noise.shape[0]
    stretch = sequence_bins * lax.axis_size("sb")
    sequence_length = stretch * lax.axis_size("sa")
    heads_key = HEADS * KEY
    heads_val = HEADS * VAL
    width = sequence_bins + 2 * BAND
    scale = KEY ** (-0.5)
    stretch_first = lax.axis_index("sa") * stretch
    first_row = stretch_first + lax.axis_index("sb") * sequence_bins
    row_pos = first_row + jnp.arange(sequence_bins, dtype=jnp.int32)
    ext_pos = first_row - BAND + jnp.arange(width, dtype=jnp.int32)
    stretch_pos = stretch_first + jnp.arange(stretch, dtype=jnp.int32)
    tiles = sequence_length // TILE
    tile_ids = jnp.arange(tiles, dtype=jnp.int32)
    pick_query = (pairs[:, 0][:, None] == tile_ids[None, :]).astype(jnp.float32)
    pick_key = (pairs[:, 1][:, None] == tile_ids[None, :]).astype(jnp.float32)
    table = jnp.dot(pick_query.T, pick_key)
    own_select = ((row_pos // TILE)[:, None] == tile_ids[None, :]).astype(jnp.float32)
    stretch_select = ((stretch_pos // TILE)[:, None] == tile_ids[None, :]).astype(jnp.float32)
    pair_own_rows = jnp.dot(jnp.dot(own_select, table), stretch_select.T) > 0.5
    pair_own_keys = jnp.dot(jnp.dot(stretch_select, table), own_select.T) > 0.5
    inside = (ext_pos >= 0) & (ext_pos < sequence_length)
    band_mask = inside[None, None, :] & (
        jnp.abs(row_pos[:, None] - ext_pos[None, :])[None] <= band_width[:, None, None]
    )
    far_rows = jnp.abs(row_pos[:, None] - stretch_pos[None, :])[None] > band_width[:, None, None]
    pair_mask = pair_own_rows[None] & far_rows
    key_mask = pair_own_keys[None] & jnp.transpose(far_rows, (0, 2, 1))
    noisy = base.astype(jnp.float32)[None] + noise.astype(jnp.float32)
    gelu_input = gelu_tanh(noisy).astype(jnp.bfloat16)
    gelu_extended = extended(gelu_input, ((("sa", "sb"), 1),), DILATION_BINS)
    hidden_state = jnp.zeros((samples_dev, sequence_bins, HID), jnp.float32)
    for tap_index in range(3):
        hidden_state = hidden_state + jnp.einsum(
            "nbd,dc->nbc",
            gelu_extended[:, tap_index * DILATION_BINS : tap_index * DILATION_BINS + sequence_bins],
            conv_full[tap_index],
            preferred_element_type=jnp.float32,
        )
    act = gelu_tanh(hidden_state).astype(jnp.bfloat16)
    resid = noisy + jnp.einsum("nbc,cd->nbd", act, mix_full, preferred_element_type=jnp.float32)
    inv_rms = lax.rsqrt(jnp.mean(resid * resid, axis=-1, keepdims=True) + 1e-06)
    normed = (resid * inv_rms * norm_gain).astype(jnp.bfloat16)
    proj = jnp.einsum("nbd,dc->nbc", normed, qkv_full, preferred_element_type=jnp.float32).astype(
        jnp.bfloat16
    )
    queries = proj[..., :heads_key].reshape(samples_dev, sequence_bins, HEADS, KEY)
    key_vals = proj[..., heads_key:]
    kv_ext = extended(key_vals, ((("sa", "sb"), 1),), BAND)
    kv_all = lax.all_gather(key_vals, "sb", axis=1, tiled=True)
    keys_ext = kv_ext[..., :heads_key].reshape(samples_dev, width, HEADS, KEY)
    vals_ext = kv_ext[..., heads_key:].reshape(samples_dev, width, HEADS, VAL)
    keys_all = kv_all[..., :heads_key].reshape(samples_dev, stretch, HEADS, KEY)
    vals_all = kv_all[..., heads_key:].reshape(samples_dev, stretch, HEADS, VAL)
    score_band = (
        jnp.einsum("nihd,njhd->nhij", queries, keys_ext, preferred_element_type=jnp.float32) * scale
    )
    score_band = jnp.where(band_mask[None], score_band, -1e30)
    raw_pair = jnp.einsum("nihd,njhd->nhij", queries, keys_all, preferred_element_type=jnp.float32)
    score_pair = jnp.where(pair_mask[None], raw_pair * scale, -1e30)
    top = jnp.maximum(jnp.max(score_band, axis=-1), jnp.max(score_pair, axis=-1))
    total = jnp.sum(jnp.where(band_mask[None], jnp.exp(score_band - top[..., None]), 0.0), axis=-1)
    total = total + jnp.sum(
        jnp.where(pair_mask[None], jnp.exp(score_pair - top[..., None]), 0.0), axis=-1
    )
    lse = top + jnp.log(total)
    prob_band = jnp.where(band_mask[None], jnp.exp(score_band - lse[..., None]), 0.0)
    prob_pair = jnp.where(pair_mask[None], jnp.exp(score_pair - lse[..., None]), 0.0)
    band_b = prob_band.astype(jnp.bfloat16)
    pair_b = prob_pair.astype(jnp.bfloat16)
    attn = jnp.einsum("nhij,njhe->nihe", band_b, vals_ext, preferred_element_type=jnp.float32)
    attn = attn + jnp.einsum(
        "nhij,njhe->nihe", pair_b, vals_all, preferred_element_type=jnp.float32
    )
    d_att = jnp.dot(cot, out_full.T, preferred_element_type=jnp.float32).astype(jnp.bfloat16)
    d_att_heads = d_att.reshape(sequence_bins, HEADS, VAL)
    delta = jnp.transpose(jnp.sum(d_att_heads.astype(jnp.float32)[None] * attn, axis=-1), (0, 2, 1))
    d_prob_band = jnp.einsum(
        "ihe,njhe->nhij", d_att_heads, vals_ext, preferred_element_type=jnp.float32
    )
    d_prob_pair = jnp.einsum(
        "ihe,njhe->nhij", d_att_heads, vals_all, preferred_element_type=jnp.float32
    )
    d_score_band = (prob_band * (d_prob_band - delta[..., None]) * scale).astype(jnp.bfloat16)
    d_score_pair = (prob_pair * (d_prob_pair - delta[..., None]) * scale).astype(jnp.bfloat16)
    d_query = jnp.einsum(
        "nhij,njhd->nihd", d_score_band, keys_ext, preferred_element_type=jnp.float32
    )
    d_query = d_query + jnp.einsum(
        "nhij,njhd->nihd", d_score_pair, keys_all, preferred_element_type=jnp.float32
    )
    d_key_ext = jnp.einsum(
        "nhij,nihd->njhd", d_score_band, queries, preferred_element_type=jnp.float32
    )
    d_val_ext = jnp.einsum(
        "nhij,ihe->njhe", band_b, d_att_heads, preferred_element_type=jnp.float32
    )
    d_kv_ext = jnp.concatenate(
        [
            d_key_ext.reshape(samples_dev, width, heads_key),
            d_val_ext.reshape(samples_dev, width, heads_val),
        ],
        axis=2,
    )
    from_right = from_behind(d_kv_ext[:, :BAND].astype(jnp.bfloat16), ("sa", "sb"), -1).astype(
        jnp.float32
    )
    from_left = from_behind(
        d_kv_ext[:, BAND + sequence_bins :].astype(jnp.bfloat16), ("sa", "sb"), 1
    ).astype(jnp.float32)
    d_key_vals = d_kv_ext[:, BAND : BAND + sequence_bins]
    d_key_vals = d_key_vals + from_left
    d_key_vals = d_key_vals + from_right
    statistics = jnp.stack([lse, delta], axis=1)
    query_rows = proj[..., :heads_key]
    queries_all, d_att_all = (
        lax.all_gather(query_rows, "sb", axis=1, tiled=True),
        lax.all_gather(d_att, "sb", axis=0, tiled=True),
    )
    stats_all = lax.all_gather(statistics, "sb", axis=3, tiled=True)
    queries_all = queries_all.reshape(samples_dev, stretch, HEADS, KEY)
    d_att_all = d_att_all.reshape(stretch, HEADS, VAL)
    keys_own = key_vals[..., :heads_key].reshape(samples_dev, sequence_bins, HEADS, KEY)
    vals_own = key_vals[..., heads_key:].reshape(samples_dev, sequence_bins, HEADS, VAL)
    score_key = (
        jnp.einsum("nihd,njhd->nhij", queries_all, keys_own, preferred_element_type=jnp.float32)
        * scale
    )
    prob_key = jnp.where(key_mask[None], jnp.exp(score_key - stats_all[:, 0][..., None]), 0.0)
    d_val_pair = jnp.einsum(
        "nhij,ihe->njhe",
        prob_key.astype(jnp.bfloat16),
        d_att_all,
        preferred_element_type=jnp.float32,
    )
    d_prob_key = jnp.einsum(
        "ihe,njhe->nhij", d_att_all, vals_own, preferred_element_type=jnp.float32
    )
    d_score_key = (prob_key * (d_prob_key - stats_all[:, 1][..., None]) * scale).astype(
        jnp.bfloat16
    )
    d_key_pair = jnp.einsum(
        "nhij,nihd->njhd", d_score_key, queries_all, preferred_element_type=jnp.float32
    )
    d_key_vals = d_key_vals + jnp.concatenate(
        [
            d_key_pair.reshape(samples_dev, sequence_bins, heads_key),
            d_val_pair.reshape(samples_dev, sequence_bins, heads_val),
        ],
        axis=2,
    )
    d_proj = jnp.concatenate(
        [d_query.reshape(samples_dev, sequence_bins, heads_key), d_key_vals], axis=2
    ).astype(jnp.bfloat16)
    d_normed = jnp.einsum("nbc,dc->nbd", d_proj, qkv_full, preferred_element_type=jnp.float32)
    gained = norm_gain * d_normed
    d_resid = (
        cot.astype(jnp.float32)[None]
        + inv_rms * gained
        - resid * inv_rms * inv_rms * inv_rms * jnp.mean(resid * gained, axis=-1, keepdims=True)
    )
    d_act = jnp.einsum(
        "nbd,cd->nbc", d_resid.astype(jnp.bfloat16), mix_full, preferred_element_type=jnp.float32
    )
    hidden_gradient = (d_act * gelu_slope(hidden_state)).astype(jnp.bfloat16)
    gradient_extended = extended(hidden_gradient, ((("sa", "sb"), 1),), DILATION_BINS)
    d_gelu_in = jnp.zeros((samples_dev, sequence_bins, base.shape[1]), jnp.float32)
    for tap_index in range(3):
        start_offset = (2 - tap_index) * DILATION_BINS
        d_gelu_in = d_gelu_in + jnp.einsum(
            "nbc,dc->nbd",
            gradient_extended[:, start_offset : start_offset + sequence_bins],
            conv_full[tap_index],
            preferred_element_type=jnp.float32,
        )
    grads = d_resid + d_gelu_in * gelu_slope(noisy)
    summed = lax.psum(jnp.sum(grads, axis=0).astype(jnp.bfloat16), "noise").astype(jnp.float32)
    return summed / (samples_dev * lax.axis_size("noise"))


def solution(mesh):
    return jax.shard_map(
        shards,
        mesh=mesh,
        in_specs=(
            P(("sa", "sb"), None),
            P("noise", ("sa", "sb"), None),
            P(("sa", "sb"), None),
            P(None, "sa", None),
            P("sa", None),
            P(),
            P("sa", None),
            P("sa", None),
            P(),
            P(),
        ),
        out_specs=P(("sa", "sb"), None),
        check_vma=False,
    )
```

profile of v0, /device:TPU:1, one launch (start us, length us, event | category | flops | bytes accessed | tf_op | source)
XLA Modules:
  0.0 632.5 jit_solution(18089078313766101049)
XLA Ops:
  8.8 0.9 convert_element_type.75
  9.7 1.2 multiply_convert_fusion.1
  10.9 8.2 %collective-permute-start.1 = (bf16[2,16,1536]{2,1,0:T(8,128)(2,1)S(1)}, bf16[2,16,1536]{2,1,0:T(8,128)(2,1)S(1)}, u32[]{:S(2)}, u32[]{:S(2)}) collective-permute-start(bf16[2,16,1536]{2,1,0:T(8,128)(2,1)S(1)} %get-tuple-element.10), channel_id=1, source_target_pairs={{2,0},{4,2},{6,4},{8,6},{10,8},{12,10},{14,12},{16,14},{18,16},{20... | collective-permute-start | bytes 294920 | tf_op jit(solution)/shard_map/ppermute | solution.py:25
  19.1 1.9 collective-permute-start
  22.6 95.0 %all-gather.6.cloned.1.call-done = bf16[3,1536,384]{2,1,0:T(8,128)(2,1)} async-done(((bf16[3,96,384]{2,1,0:T(8,128)(2,1)}), bf16[3,1536,384]{2,1,0:T(8,128)(2,1)}) %all-gather.6.cloned.1.call-update) | async-done | bytes 3538960 | tf_op jit(solution)/shard_map/all_gather | solution.py:50
  117.6 1.6 fusion.58
  119.2 1.6 fusion.60
  120.8 1.6 fusion.44
  122.4 97.1 %all-gather.8.cloned.1.call-done = bf16[384,1536]{1,0:T(8,128)(2,1)} async-done(((bf16[24,1536]{1,0:T(8,128)(2,1)}), bf16[384,1536]{1,0:T(8,128)(2,1)}) %all-gather.8.cloned.1.call-update) | async-done | bytes 1179664 | tf_op jit(solution)/shard_map/all_gather | solution.py:51
  219.5 1.7 multiply_reduce_fusion.1
  221.2 103.6 %all-gather.10.cloned.1.call-done = bf16[1536,896]{1,0:T(8,128)(2,1)} async-done(((bf16[96,896]{1,0:T(8,128)(2,1)}), bf16[1536,896]{1,0:T(8,128)(2,1)}) %all-gather.10.cloned.1.call-update) | async-done | bytes 2752528 | tf_op jit(solution)/shard_map/all_gather | solution.py:52
  324.9 2.4 fusion.28
  329.6 96.9 %all-gather.14.cloned.1.call-done = bf16[384,1536]{1,0:T(8,128)(2,1)} async-done(((bf16[24,1536]{1,0:T(8,128)(2,1)}), bf16[384,1536]{1,0:T(8,128)(2,1)}) %all-gather.14.cloned.1.call-update) | async-done | bytes 1179664 | tf_op jit(solution)/shard_map/all_gather | solution.py:53
  426.5 1.7 convolution_convert_fusion
  428.9 18.8 %all_gather.31 = bf16[512,384]{1,0:T(8,128)(2,1)S(1)} all-gather(bf16[32,384]{1,0:T(8,128)(2,1)S(1)} %convolution_convert_fusion), channel_id=1, replica_groups=mesh['sa'=16,'sb'=16,'noise'=2] {'sb'}, dimensions={0}, use_global_device_ids=true | all-gather | bytes 417792 | tf_op jit(solution)/shard_map/all_gather | solution.py:173
  447.9 2.7 collective-permute-start.2
  450.7 9.8 %collective-permute-start.3 = (bf16[2,32,640]{2,1,0:T(8,128)(2,1)S(1)}, bf16[2,32,640]{2,1,0:T(8,128)(2,1)S(1)}, u32[]{:S(2)}, u32[]{:S(2)}) collective-permute-start(bf16[2,32,640]{2,1,0:T(8,128)(2,1)S(1)} %copy-done.11), channel_id=1, source_target_pairs={{2,0},{4,2},{6,4},{8,6},{10,8},{12,10},{14,12},{16,14},{18,16},{20... | collective-permute-start | bytes 245768 | tf_op jit(solution)/shard_map/ppermute | solution.py:25
  460.6 16.1 %all_gather.29 = bf16[2,512,256]{2,1,0:T(8,128)(2,1)S(1)} all-gather(bf16[2,32,256]{2,1,0:T(8,128)(2,1)S(1)} %get-tuple-element.12), channel_id=1, replica_groups=mesh['sa'=16,'sb'=16,'noise'=2] {'sb'}, dimensions={1}, use_global_device_ids=true | all-gather | bytes 557056 | tf_op jit(solution)/shard_map/all_gather | solution.py:172
  476.9 0.8 reshape.249
  478.6 0.8 reshape.242
  479.7 9.0 %all-gather.12.cloned.1.call-done = bf16[2,512,640]{2,1,0:T(8,128)(2,1)} async-done(((bf16[2,32,640]{2,1,0:T(8,128)(2,1)}), bf16[2,512,640]{2,1,0:T(8,128)(2,1)}) %all-gather.12.cloned.1.call-update) | async-done | bytes 1310736 | tf_op jit(solution)/shard_map/all_gather | solution.py:105
  488.7 1.0 slice-done
  490.3 0.8 select_reduce_fusion
  491.1 0.8 select_reduce_fusion.1
  493.0 1.3 fusion.70
  494.3 0.9 fusion.50
  495.3 1.9 fusion.26
  497.2 1.0 fusion.45
  499.1 19.1 %all_gather.30 = f32[2,2,4,512]{2,1,0,3:T(2,128)S(1)} all-gather(f32[2,2,4,32]{2,1,0,3:T(2,128)S(1)} %copy.131), channel_id=1, replica_groups=mesh['sa'=16,'sb'=16,'noise'=2] {'sb'}, dimensions={3}, use_global_device_ids=true | all-gather | bytes 34816 | tf_op jit(solution)/shard_map/all_gather | solution.py:175
  518.1 0.8 fusion.150
  519.2 0.8 copy.135
  521.9 2.0 collective-permute-start.4
  523.9 10.6 %collective-permute-start.5 = (bf16[2,32,640]{2,1,0:T(8,128)(2,1)}, bf16[2,32,640]{2,1,0:T(8,128)(2,1)}, u32[]{:S(2)}, u32[]{:S(2)}) collective-permute-start(bf16[2,32,640]{2,1,0:T(8,128)(2,1)} %get-tuple-element.8), channel_id=1, source_target_pairs={{2,0},{4,2},{6,4},{8,6},{10,8},{12,10},{14,12},{16,14},{18,16},{20... | collective-permute-start | bytes 245768 | tf_op jit(solution)/shard_map/ppermute | solution.py:33
  534.6 1.1 fusion.157
  535.6 0.9 convolution_bitcast_fusion.3
  536.5 2.5 fusion.31
  539.0 1.2 fusion.51
  541.0 1.6 copy.136
  542.6 1.7 reshape.252
  544.3 1.6 copy.138
  545.9 1.0 reshape.253
  547.0 1.1 fusion.94
  548.2 2.0 multiply_reduce_fusion
  550.7 1.9 collective-permute-start.7
  552.6 7.0 %collective-permute-start.6 = (bf16[2,16,384]{2,1,0:T(8,128)(2,1)S(1)}, bf16[2,16,384]{2,1,0:T(8,128)(2,1)S(1)}, u32[]{:S(2)}, u32[]{:S(2)}) collective-permute-start(bf16[2,16,384]{2,1,0:T(8,128)(2,1)S(1)} %get-tuple-element.13), channel_id=1, source_target_pairs={{2,0},{4,2},{6,4},{8,6},{10,8},{12,10},{14,12},{16,14},{18,16},{20... | collective-permute-start | bytes 73736 | tf_op jit(solution)/shard_map/ppermute | solution.py:25
  561.1 1.3 fusion.25
  562.4 61.6 %all-reduce.2.cloned.1.call-done = bf16[32,1536]{1,0:T(8,128)(2,1)} async-done(((bf16[32,1536]{1,0:T(8,128)(2,1)}), bf16[32,1536]{1,0:T(8,128)(2,1)}) %all-reduce.2.cloned.1.call-update) | async-done | bytes 98320 | tf_op jit(solution)/shard_map/psum | solution.py:232
  624.0 1.6 convert_multiply_fusion
  (158 shorter events, 15.6 us)
Async XLA Ops:
  6.5 14.7 %copy-start.40 = (s32[64,2]{0,1:T(2,128)S(1)}, s32[64,2]{0,1:T(2,128)}, u32[]{:S(2)}) copy-start(s32[64,2]{0,1:T(2,128)} %param.19) | copy-start | bytes 1540
  6.5 14.7 %copy-start.24 = (bf16[32,1536]{1,0:T(8,128)(2,1)S(1)}, bf16[32,1536]{1,0:T(8,128)(2,1)}, u32[]{:S(2)}) copy-start(bf16[32,1536]{1,0:T(8,128)(2,1)} %param.12) | copy-start | bytes 294916
  6.5 111.0 %all-gather.6.cloned.1.call-start = ((), (), s32[]{:S(2)}) async-start(), calls=%async_computation | async-start | bytes 3760128 | tf_op jit(solution)/shard_map/all_gather | solution.py:50
  7.3 212.3 %all-gather.8.cloned.1.call-start = ((), (), s32[]{:S(2)}) async-start(), calls=%async_computation.1 | async-start | bytes 1253376 | tf_op jit(solution)/shard_map/all_gather | solution.py:51
  8.0 316.8 %all-gather.10.cloned.1.call-start = ((), (), s32[]{:S(2)}) async-start(), calls=%async_computation.2 | async-start | bytes 2924544 | tf_op jit(solution)/shard_map/all_gather | solution.py:52
  8.7 417.7 %all-gather.14.cloned.1.call-start = ((), (), s32[]{:S(2)}) async-start(), calls=%async_computation.4 | async-start | bytes 1253376 | tf_op jit(solution)/shard_map/all_gather | solution.py:53
  9.7 209.8 %copy-start.8 = (f32[32,1536]{1,0:T(8,128)}, f32[32,1536]{1,0:T(8,128)S(1)}, u32[]{:S(2)}) copy-start(f32[32,1536]{1,0:T(8,128)S(1)} %convert_element_type.75) | copy-start | bytes 589828
  10.9 108.3 %collective-permute-start.1 = (bf16[2,16,1536]{2,1,0:T(8,128)(2,1)S(1)}, bf16[2,16,1536]{2,1,0:T(8,128)(2,1)S(1)}, u32[]{:S(2)}, u32[]{:S(2)}) collective-permute-start(bf16[2,16,1536]{2,1,0:T(8,128)(2,1)S(1)} %get-tuple-element.10), channel_id=1, source_target_pairs={{2,0},{4,2},{6,4},{8,6},{10,8},{12,10},{14,12},{16,14},{18,16},{20... | collective-permute-start | bytes 294920 | tf_op jit(solution)/shard_map/ppermute | solution.py:25
  19.1 101.7 %collective-permute-start = (bf16[2,16,1536]{2,1,0:T(8,128)(2,1)S(1)}, bf16[2,16,1536]{2,1,0:T(8,128)(2,1)S(1)}, u32[]{:S(2)}, u32[]{:S(2)}) collective-permute-start(bf16[2,16,1536]{2,1,0:T(8,128)(2,1)S(1)} %get-tuple-element.9), channel_id=1, source_target_pairs={{0,2},{2,4},{4,6},{6,8},{8,10},{10,12},{12,14},{14,16},{16,18},{18... | collective-permute-start | bytes 294920 | tf_op jit(solution)/shard_map/ppermute | solution.py:24
  21.1 467.6 %all-gather.12.cloned.1.call-start = ((), (), s32[]{:S(2)}) async-start(), calls=%async_computation.3 | async-start | bytes 1392640 | tf_op jit(solution)/shard_map/all_gather | solution.py:105
  120.8 98.8 %copy-start.20 = (bf16[2,32,1536]{2,1,0:T(8,128)(2,1)S(1)}, bf16[2,32,1536]{2,1,0:T(8,128)(2,1)}, u32[]{:S(2)}) copy-start(bf16[2,32,1536]{2,1,0:T(8,128)(2,1)} %param.11) | copy-start | bytes 589828
  122.4 204.9 %copy-start.17 = (f32[2,32,384]{2,1,0:T(8,128)}, f32[2,32,384]{2,1,0:T(8,128)S(1)}, u32[]{:S(2)}) copy-start(f32[2,32,384]{2,1,0:T(8,128)S(1)} %fusion.44) | copy-start | bytes 294916
  122.4 202.4 %copy-start.31 = (f32[1536]{0:T(1024)S(1)}, f32[1536]{0:T(1024)}, u32[]{:S(2)}) copy-start(f32[1536]{0:T(1024)} %param.15) | copy-start | bytes 18436
  221.2 106.1 %copy-start.37 = (f32[2,32]{1,0:T(2,128)}, f32[2,32]{1,0:T(2,128)S(1)}, u32[]{:S(2)}) copy-start(f32[2,32]{1,0:T(2,128)S(1)} %add_rsqrt_fusion) | copy-start | bytes 772
  324.9 3.2 copy-start.39
  327.3 133.1 %copy-start.19 = (bf16[2,32,896]{2,1,0:T(8,128)(2,1)}, bf16[2,32,896]{2,1,0:T(8,128)(2,1)S(1)}, u32[]{:S(2)}) copy-start(bf16[2,32,896]{2,1,0:T(8,128)(2,1)S(1)} %fusion.28) | copy-start | bytes 344068
  328.0 296.1 %all-reduce.2.cloned.1.call-start = ((), (), s32[]{:S(2)}) async-start(), calls=%async_computation.5 | async-start | bytes 196608 | tf_op jit(solution)/shard_map/psum | solution.py:232
  328.9 161.4 %copy-start.13 = (pred[4,32,512]{2,1,0:T(8,128)(4,1)}, pred[4,32,512]{2,1,0:T(8,128)(4,1)S(1)}, u32[]{:S(2)}) copy-start(pred[4,32,512]{2,1,0:T(8,128)(4,1)S(1)} %compare_and_fusion.1) | copy-start | bytes 196612
  329.6 118.3 %copy-start.11 = (bf16[2,32,640]{2,1,0:T(8,128)(2,1)S(1)}, bf16[2,32,640]{2,1,0:T(8,128)(2,1)}, u32[]{:S(2)}) copy-start(bf16[2,32,640]{2,1,0:T(8,128)(2,1)} %slice.121) | copy-start | bytes 245764
  428.3 19.4 %copy-start.25 = (bf16[32,4,96]{2,1,0:T(4,128)(2,1)}, bf16[32,4,96]{2,1,0:T(4,128)(2,1)S(1)}, u32[]{:S(2)}) copy-start(bf16[32,4,96]{2,1,0:T(4,128)(2,1)S(1)} %reshape.243) | copy-start | bytes 73732
  447.9 30.5 %collective-permute-start.2 = (bf16[2,32,640]{2,1,0:T(8,128)(2,1)S(1)}, bf16[2,32,640]{2,1,0:T(8,128)(2,1)S(1)}, u32[]{:S(2)}, u32[]{:S(2)}) collective-permute-start(bf16[2,32,640]{2,1,0:T(8,128)(2,1)S(1)} %copy-done.11), channel_id=1, source_target_pairs={{0,2},{2,4},{4,6},{6,8},{8,10},{10,12},{12,14},{14,16},{16,18},{18... | collective-permute-start | bytes 245768 | tf_op jit(solution)/shard_map/ppermute | solution.py:24
  450.7 27.8 %collective-permute-start.3 = (bf16[2,32,640]{2,1,0:T(8,128)(2,1)S(1)}, bf16[2,32,640]{2,1,0:T(8,128)(2,1)S(1)}, u32[]{:S(2)}, u32[]{:S(2)}) collective-permute-start(bf16[2,32,640]{2,1,0:T(8,128)(2,1)S(1)} %copy-done.11), channel_id=1, source_target_pairs={{2,0},{4,2},{6,4},{8,6},{10,8},{12,10},{14,12},{16,14},{18,16},{20... | collective-permute-start | bytes 245768 | tf_op jit(solution)/shard_map/ppermute | solution.py:25
  460.5 17.2 %slice-start.2 = ((bf16[2,32,896]{2,1,0:T(8,128)(2,1)}), bf16[2,32,384]{2,1,0:T(8,128)(2,1)S(1)}, s32[]{:S(2)}) async-start(bf16[2,32,896]{2,1,0:T(8,128)(2,1)} %copy-done.19), calls=%async_computation.8 | async-start | bytes 98304 | tf_op jit(solution)/shard_map/slice | solution.py:179
  460.6 29.4 %copy-start.15 = (bf16[2,32,4,64]{3,2,1,0:T(4,128)(2,1)}, bf16[2,32,4,64]{3,2,1,0:T(4,128)(2,1)S(1)}, u32[]{:S(2)}) copy-start(bf16[2,32,4,64]{3,2,1,0:T(4,128)(2,1)S(1)} %reshape.240) | copy-start | bytes 98308
  476.9 57.6 %copy-start.2 = (bf16[2,512,256]{1,2,0:T(8,128)(2,1)}, bf16[2,512,256]{1,2,0:T(8,128)(2,1)S(1)}, u32[]{:S(2)}) copy-start(bf16[2,512,256]{1,2,0:T(8,128)(2,1)S(1)} %copy.129) | copy-start | bytes 1572868
  478.6 11.4 %copy-start.12 = (bf16[2,96,256]{1,2,0:T(8,128)(2,1)}, bf16[2,96,256]{1,2,0:T(8,128)(2,1)S(1)}, u32[]{:S(2)}) copy-start(bf16[2,96,256]{1,2,0:T(8,128)(2,1)S(1)} %copy.113) | copy-start | bytes 294916
  492.2 2.1 copy-start.22
  492.2 2.1 copy-start.29
  492.2 3.0 copy-start.7
  492.3 3.0 copy-start.14
  493.0 2.2 copy-start.33
  498.2 21.8 %copy-start.30 = (bf16[2,4,32,96]{3,2,1,0:T(8,128)(2,1)}, bf16[2,4,32,96]{3,2,1,0:T(8,128)(2,1)S(1)}, u32[]{:S(2)}) copy-start(bf16[2,4,32,96]{3,2,1,0:T(8,128)(2,1)S(1)} %fusion.45) | copy-start | bytes 147460
  520.7 13.9 %copy-start.27 = (pred[4,512,32]{1,2,0:T(8,128)(4,1)S(1)}, pred[4,512,32]{1,2,0:T(8,128)(4,1)}, u32[]{:S(2)}) copy-start(pred[4,512,32]{1,2,0:T(8,128)(4,1)} %compare_and_fusion) | copy-start | bytes 196612
  520.7 13.9 %copy-start.28 = (bf16[2,32,4,64]{3,2,1,0:T(4,128)(2,1)S(1)}, bf16[2,32,4,64]{3,2,1,0:T(4,128)(2,1)}, u32[]{:S(2)}) copy-start(bf16[2,32,4,64]{3,2,1,0:T(4,128)(2,1)} %reshape.249) | copy-start | bytes 98308
  521.1 14.5 %copy-start.4 = (f32[2,96,384]{2,1,0:T(8,128)}, f32[2,96,384]{2,1,0:T(8,128)S(1)}, u32[]{:S(2)}) copy-start(f32[2,96,384]{2,1,0:T(8,128)S(1)} %reshape.247) | copy-start | bytes 884740
  521.9 14.7 %copy-start.35 = (f32[2,4,512]{2,1,0:T(4,128)S(1)}, f32[2,4,512]{2,1,0:T(4,128)}, u32[]{:S(2)}) copy-start(f32[2,4,512]{2,1,0:T(4,128)} %copy.135) | copy-start | bytes 49156
  521.9 25.1 %collective-permute-start.4 = (bf16[2,32,640]{2,1,0:T(8,128)(2,1)}, bf16[2,32,640]{2,1,0:T(8,128)(2,1)}, u32[]{:S(2)}, u32[]{:S(2)}) collective-permute-start(bf16[2,32,640]{2,1,0:T(8,128)(2,1)} %get-tuple-element.7), channel_id=1, source_target_pairs={{0,2},{2,4},{4,6},{6,8},{8,10},{10,12},{12,14},{14,16},{16,18},{18... | collective-permute-start | bytes 245768 | tf_op jit(solution)/shard_map/ppermute | solution.py:33
  523.9 23.1 %collective-permute-start.5 = (bf16[2,32,640]{2,1,0:T(8,128)(2,1)}, bf16[2,32,640]{2,1,0:T(8,128)(2,1)}, u32[]{:S(2)}, u32[]{:S(2)}) collective-permute-start(bf16[2,32,640]{2,1,0:T(8,128)(2,1)} %get-tuple-element.8), channel_id=1, source_target_pairs={{2,0},{4,2},{6,4},{8,6},{10,8},{12,10},{14,12},{16,14},{18,16},{20... | collective-permute-start | bytes 245768 | tf_op jit(solution)/shard_map/ppermute | solution.py:33
  536.5 11.6 %copy-start = (bf16[1536,896]{1,0:T(8,128)(2,1)S(1)}, bf16[1536,896]{1,0:T(8,128)(2,1)}, u32[]{:S(2)}) copy-start(bf16[1536,896]{1,0:T(8,128)(2,1)} %all-gather.10.cloned.1.call-done) | copy-start | bytes 8257540
  539.0 8.0 %copy-start.5 = (f32[2,96,384]{2,1,0:T(8,128)S(1)}, f32[2,96,384]{2,1,0:T(8,128)}, u32[]{:S(2)}) copy-start(f32[2,96,384]{2,1,0:T(8,128)} %copy-done.4) | copy-start | bytes 884740
  539.0 9.1 %copy-start.32 = (f32[1536]{0:T(1024)S(1)}, f32[1536]{0:T(1024)}, u32[]{:S(2)}) copy-start(f32[1536]{0:T(1024)} %param.15) | copy-start | bytes 18436
  547.0 3.1 copy-start.18
  547.0 3.1 copy-start.23
  547.0 3.1 copy-start.38
  548.1 2.0 copy-start.1
  548.1 11.5 %copy-start.3 = (bf16[3,1536,384]{2,1,0:T(8,128)(2,1)S(1)}, bf16[3,1536,384]{2,1,0:T(8,128)(2,1)}, u32[]{:S(2)}) copy-start(bf16[3,1536,384]{2,1,0:T(8,128)(2,1)} %all-gather.6.cloned.1.call-done) | copy-start | bytes 10616836
  550.7 9.4 %collective-permute-start.7 = (bf16[2,16,384]{2,1,0:T(8,128)(2,1)S(1)}, bf16[2,16,384]{2,1,0:T(8,128)(2,1)S(1)}, u32[]{:S(2)}, u32[]{:S(2)}) collective-permute-start(bf16[2,16,384]{2,1,0:T(8,128)(2,1)S(1)} %get-tuple-element.14), channel_id=1, source_target_pairs={{0,2},{2,4},{4,6},{6,8},{8,10},{10,12},{12,14},{14,16},{16,18},{18... | collective-permute-start | bytes 73736 | tf_op jit(solution)/shard_map/ppermute | solution.py:24
  552.6 8.0 %collective-permute-start.6 = (bf16[2,16,384]{2,1,0:T(8,128)(2,1)S(1)}, bf16[2,16,384]{2,1,0:T(8,128)(2,1)S(1)}, u32[]{:S(2)}, u32[]{:S(2)}) collective-permute-start(bf16[2,16,384]{2,1,0:T(8,128)(2,1)S(1)} %get-tuple-element.13), channel_id=1, source_target_pairs={{2,0},{4,2},{6,4},{8,6},{10,8},{12,10},{14,12},{16,14},{18,16},{20... | collective-permute-start | bytes 73736 | tf_op jit(solution)/shard_map/ppermute | solution.py:25
  (10 other events, 13.8 us)
Sparse Core Ops, SparseCore 0:
  9.4 108.0 all-gather.5
  119.6 99.8 all-gather.7
  221.6 103.1 all-gather.9
  326.8 99.6 all-gather.13
  429.3 59.3 all-gather.11
  562.6 61.4 all-reduce.1
where the time goes:
time: 634 us; the launch traced here: 632 us
  waiting for transfers between devices  465 us (73%)
  blocking collectives  53.9 us (9%)
  starting transfers between devices  44.4 us (7%)
  matrix products  28.2 us (4%)
  local copies, waits for them, and re-layouts  16.6 us (3%)
  between operations  14.4 us (2%)
  other arithmetic  9.81 us (2%)
    all_gather x1, waiting for transfers between devices, shards(): lax.all_gather(qkv_w, 'sa', axis=0, tiled=True)  104 us
    all_gather x1, waiting for transfers between devices, shards(): lax.all_gather(mix_w, 'sa', axis=0, tiled=True)  97.1 us
    all_gather x1, waiting for transfers between devices, shards(): lax.all_gather(out_w, 'sa', axis=0, tiled=True)  96.9 us
    all_gather x1, waiting for transfers between devices, shards(): lax.all_gather(convolution_weight, 'sa', axis=1, tiled=True)  95 us
    psum x1, waiting for transfers between devices, shards(): lax.psum(jnp.sum(grads, axis=0).astype(jnp.bfloat16), 'noise')  61.6 us
    ppermute x3, starting transfers between devices, extended(): after = lax.ppermute(leading, axis, down)  25 us
    all_gather x1, blocking collectives, shards(): stats_all = lax.all_gather(statistics, 'sb', axis=3, tiled=True)  19.1 us
    all_gather x1, blocking collectives, shards(): lax.all_gather(d_att, 'sb', axis=0, tiled=True)  18.8 us
  transfers between devices with their start and end apart: 14, of which 6 were waited for; matrix products, arithmetic and copies ran while one was open for 5% of the time, Pallas kernels for 0%

commit v1 on v0

--- a/solution.py
+++ b/solution.py
@@ -229,7 +229,9 @@
             preferred_element_type=jnp.float32,
         )
     grads = d_resid + d_gelu_in * gelu_slope(noisy)
-    summed = lax.psum(jnp.sum(grads, axis=0).astype(jnp.bfloat16), "noise").astype(jnp.float32)
+    summed = jnp.sum(
+        lax.all_gather(jnp.sum(grads, axis=0).astype(jnp.bfloat16), "noise"), axis=0
+    ).astype(jnp.float32)
     return summed / (samples_dev * lax.axis_size("noise"))
 
 

time: 634 us -> 591 us (0.932); the launches traced: 632 us -> 583 us
  waiting for transfers between devices: 465 us -> 404 us
  blocking collectives: 53.9 us -> 67.5 us
    psum x1 -> x0, waiting for transfers between devices: 61.6 us -> none  [shards(): lax.psum(jnp.sum(grads, axis=0).astype(jnp.bfloat16), 'noise')]
    all_gather x0 -> x1, blocking collectives: none -> 13.8 us  [shards(): lax.all_gather(jnp.sum(grads, axis=0).astype(jnp.bfloat16), 'noise')]
  transfers between devices with their start and end apart: 14 -> 13, of which waited for: 6 -> 5; matrix products, arithmetic and copies ran while one was open for 5% -> 6% of each run, Pallas kernels for 0% -> 0%
where the time goes in v1:
time: 591 us; the launch traced here: 583 us
  waiting for transfers between devices  404 us (68%)
  blocking collectives  67.5 us (11%)
  starting transfers between devices  44.8 us (8%)
  matrix products  27.5 us (5%)
  local copies, waits for them, and re-layouts  16.5 us (3%)
  between operations  14.1 us (2%)
  other arithmetic  8.96 us (2%)
    all_gather x1, waiting for transfers between devices, shards(): lax.all_gather(qkv_w, 'sa', axis=0, tiled=True)  104 us
    all_gather x1, waiting for transfers between devices, shards(): lax.all_gather(mix_w, 'sa', axis=0, tiled=True)  97.1 us
    all_gather x1, waiting for transfers between devices, shards(): lax.all_gather(out_w, 'sa', axis=0, tiled=True)  96.9 us
    all_gather x1, waiting for transfers between devices, shards(): lax.all_gather(convolution_weight, 'sa', axis=1, tiled=True)  95 us
    ppermute x3, starting transfers between devices, extended(): after = lax.ppermute(leading, axis, down)  25 us
    all_gather x1, blocking collectives, shards(): stats_all = lax.all_gather(statistics, 'sb', axis=3, tiled=True)  18.9 us
    all_gather x1, blocking collectives, shards(): lax.all_gather(d_att, 'sb', axis=0, tiled=True)  18.8 us
    all_gather x1, blocking collectives, shards(): lax.all_gather(query_rows, 'sb', axis=1, tiled=True)  16.1 us
  transfers between devices with their start and end apart: 13, of which 5 were waited for; matrix products, arithmetic and copies ran while one was open for 6% of the time, Pallas kernels for 0%

profile of v1, /device:TPU:1, one launch (start us, length us, event | category | flops | bytes accessed | tf_op | source)
XLA Modules:
  0.0 583.1 jit_solution(5853787161461716855)
XLA Ops:
  8.8 0.9 convert_element_type.87
  9.7 1.2 multiply_convert_fusion.1
  10.9 8.2 %collective-permute-start.1 = (bf16[2,16,1536]{2,1,0:T(8,128)(2,1)S(1)}, bf16[2,16,1536]{2,1,0:T(8,128)(2,1)S(1)}, u32[]{:S(2)}, u32[]{:S(2)}) collective-permute-start(bf16[2,16,1536]{2,1,0:T(8,128)(2,1)S(1)} %get-tuple-element.10), channel_id=1, source_target_pairs={{2,0},{4,2},{6,4},{8,6},{10,8},{12,10},{14,12},{16,14},{18,16},{20... | collective-permute-start | bytes 294920 | tf_op jit(solution)/shard_map/ppermute | solution.py:25
  19.1 1.9 collective-permute-start
  22.6 95.0 %all-gather.7.cloned.1.call-done = bf16[3,1536,384]{2,1,0:T(8,128)(2,1)} async-done(((bf16[3,96,384]{2,1,0:T(8,128)(2,1)}), bf16[3,1536,384]{2,1,0:T(8,128)(2,1)}) %all-gather.7.cloned.1.call-update) | async-done | bytes 3538960 | tf_op jit(solution)/shard_map/all_gather | solution.py:50
  117.6 1.6 fusion.58
  119.2 1.6 fusion.60
  120.8 1.6 fusion.44
  122.4 97.1 %all-gather.9.cloned.1.call-done = bf16[384,1536]{1,0:T(8,128)(2,1)} async-done(((bf16[24,1536]{1,0:T(8,128)(2,1)}), bf16[384,1536]{1,0:T(8,128)(2,1)}) %all-gather.9.cloned.1.call-update) | async-done | bytes 1179664 | tf_op jit(solution)/shard_map/all_gather | solution.py:51
  219.5 1.7 multiply_reduce_fusion.1
  221.2 103.6 %all-gather.11.cloned.1.call-done = bf16[1536,896]{1,0:T(8,128)(2,1)} async-done(((bf16[96,896]{1,0:T(8,128)(2,1)}), bf16[1536,896]{1,0:T(8,128)(2,1)}) %all-gather.11.cloned.1.call-update) | async-done | bytes 2752528 | tf_op jit(solution)/shard_map/all_gather | solution.py:52
  324.9 2.4 fusion.28
  328.8 0.7 compare_and_fusion
  329.5 96.9 %all-gather.15.cloned.1.call-done = bf16[384,1536]{1,0:T(8,128)(2,1)} async-done(((bf16[24,1536]{1,0:T(8,128)(2,1)}), bf16[384,1536]{1,0:T(8,128)(2,1)}) %all-gather.15.cloned.1.call-update) | async-done | bytes 1179664 | tf_op jit(solution)/shard_map/all_gather | solution.py:53
  426.5 1.7 convolution_convert_fusion
  428.9 18.8 %all_gather.35 = bf16[512,384]{1,0:T(8,128)(2,1)S(1)} all-gather(bf16[32,384]{1,0:T(8,128)(2,1)S(1)} %convolution_convert_fusion), channel_id=1, replica_groups=mesh['sa'=16,'sb'=16,'noise'=2] {'sb'}, dimensions={0}, use_global_device_ids=true | all-gather | bytes 417792 | tf_op jit(solution)/shard_map/all_gather | solution.py:173
  447.9 2.7 collective-permute-start.2
  450.6 9.8 %collective-permute-start.3 = (bf16[2,32,640]{2,1,0:T(8,128)(2,1)S(1)}, bf16[2,32,640]{2,1,0:T(8,128)(2,1)S(1)}, u32[]{:S(2)}, u32[]{:S(2)}) collective-permute-start(bf16[2,32,640]{2,1,0:T(8,128)(2,1)S(1)} %copy-done.11), channel_id=1, source_target_pairs={{2,0},{4,2},{6,4},{8,6},{10,8},{12,10},{14,12},{16,14},{18,16},{20... | collective-permute-start | bytes 245768 | tf_op jit(solution)/shard_map/ppermute | solution.py:25
  460.6 16.1 %all_gather.33 = bf16[2,512,256]{2,1,0:T(8,128)(2,1)S(1)} all-gather(bf16[2,32,256]{2,1,0:T(8,128)(2,1)S(1)} %get-tuple-element.12), channel_id=1, replica_groups=mesh['sa'=16,'sb'=16,'noise'=2] {'sb'}, dimensions={1}, use_global_device_ids=true | all-gather | bytes 557056 | tf_op jit(solution)/shard_map/all_gather | solution.py:172
  476.9 0.8 reshape.257
  478.6 0.8 reshape.250
  479.6 9.0 %all-gather.13.cloned.1.call-done = bf16[2,512,640]{2,1,0:T(8,128)(2,1)} async-done(((bf16[2,32,640]{2,1,0:T(8,128)(2,1)}), bf16[2,512,640]{2,1,0:T(8,128)(2,1)}) %all-gather.13.cloned.1.call-update) | async-done | bytes 1310736 | tf_op jit(solution)/shard_map/all_gather | solution.py:105
  488.7 1.0 slice-done
  490.3 0.8 select_reduce_fusion
  491.1 0.8 select_reduce_fusion.1
  492.3 0.8 log_add_fusion
  493.0 1.3 fusion.70
  494.3 0.9 fusion.50
  495.3 1.9 fusion.26
  497.2 1.0 fusion.45
  499.1 18.9 %all_gather.34 = f32[2,2,4,512]{2,1,0,3:T(2,128)S(1)} all-gather(f32[2,2,4,32]{2,1,0,3:T(2,128)S(1)} %copy.131), channel_id=1, replica_groups=mesh['sa'=16,'sb'=16,'noise'=2] {'sb'}, dimensions={3}, use_global_device_ids=true | all-gather | bytes 34816 | tf_op jit(solution)/shard_map/all_gather | solution.py:175
  518.0 0.8 fusion.150
  519.0 0.8 copy.135
  521.7 2.0 collective-permute-start.4
  523.8 11.0 %collective-permute-start.5 = (bf16[2,32,640]{2,1,0:T(8,128)(2,1)}, bf16[2,32,640]{2,1,0:T(8,128)(2,1)}, u32[]{:S(2)}, u32[]{:S(2)}) collective-permute-start(bf16[2,32,640]{2,1,0:T(8,128)(2,1)} %get-tuple-element.8), channel_id=1, source_target_pairs={{2,0},{4,2},{6,4},{8,6},{10,8},{12,10},{14,12},{16,14},{18,16},{20... | collective-permute-start | bytes 245768 | tf_op jit(solution)/shard_map/ppermute | solution.py:33
  534.8 1.0 fusion.157
  535.9 0.9 convolution_bitcast_fusion.3
  536.8 2.5 fusion.31
  539.3 1.2 fusion.51
  541.2 1.6 copy.136
  542.9 1.7 reshape.260
  544.6 1.6 copy.138
  546.2 1.0 reshape.261
  547.3 1.1 fusion.94
  548.4 2.0 multiply_reduce_fusion
  551.0 1.9 collective-permute-start.7
  552.9 7.0 %collective-permute-start.6 = (bf16[2,16,384]{2,1,0:T(8,128)(2,1)S(1)}, bf16[2,16,384]{2,1,0:T(8,128)(2,1)S(1)}, u32[]{:S(2)}, u32[]{:S(2)}) collective-permute-start(bf16[2,16,384]{2,1,0:T(8,128)(2,1)S(1)} %get-tuple-element.13), channel_id=1, source_target_pairs={{2,0},{4,2},{6,4},{8,6},{10,8},{12,10},{14,12},{16,14},{18,16},{20... | collective-permute-start | bytes 73736 | tf_op jit(solution)/shard_map/ppermute | solution.py:25
  562.0 13.8 %all-gather = bf16[64,1536]{1,0:T(8,128)(2,1)S(1)} all-gather(bf16[32,1536]{1,0:T(8,128)(2,1)S(1)} %fusion.25), channel_id=2, replica_groups=mesh['sa'=16,'sb'=16,'noise'=2] {'noise'}, dimensions={0}, use_global_device_ids=true | all-gather | bytes 294912 | tf_op jit(solution)/shard_map/all_gather | solution.py:233
  (157 shorter events, 15.4 us)
Async XLA Ops:
  6.5 14.7 %copy-start.40 = (s32[64,2]{0,1:T(2,128)S(1)}, s32[64,2]{0,1:T(2,128)}, u32[]{:S(2)}) copy-start(s32[64,2]{0,1:T(2,128)} %param.19) | copy-start | bytes 1540
  6.5 14.7 %copy-start.24 = (bf16[32,1536]{1,0:T(8,128)(2,1)S(1)}, bf16[32,1536]{1,0:T(8,128)(2,1)}, u32[]{:S(2)}) copy-start(bf16[32,1536]{1,0:T(8,128)(2,1)} %param.12) | copy-start | bytes 294916
  6.5 111.0 %all-gather.7.cloned.1.call-start = ((), (), s32[]{:S(2)}) async-start(), calls=%async_computation | async-start | bytes 3760128 | tf_op jit(solution)/shard_map/all_gather | solution.py:50
  7.3 212.3 %all-gather.9.cloned.1.call-start = ((), (), s32[]{:S(2)}) async-start(), calls=%async_computation.1 | async-start | bytes 1253376 | tf_op jit(solution)/shard_map/all_gather | solution.py:51
  8.0 316.8 %all-gather.11.cloned.1.call-start = ((), (), s32[]{:S(2)}) async-start(), calls=%async_computation.2 | async-start | bytes 2924544 | tf_op jit(solution)/shard_map/all_gather | solution.py:52
  8.7 417.7 %all-gather.15.cloned.1.call-start = ((), (), s32[]{:S(2)}) async-start(), calls=%async_computation.4 | async-start | bytes 1253376 | tf_op jit(solution)/shard_map/all_gather | solution.py:53
  9.7 209.8 %copy-start.8 = (f32[32,1536]{1,0:T(8,128)}, f32[32,1536]{1,0:T(8,128)S(1)}, u32[]{:S(2)}) copy-start(f32[32,1536]{1,0:T(8,128)S(1)} %convert_element_type.87) | copy-start | bytes 589828
  10.9 108.3 %collective-permute-start.1 = (bf16[2,16,1536]{2,1,0:T(8,128)(2,1)S(1)}, bf16[2,16,1536]{2,1,0:T(8,128)(2,1)S(1)}, u32[]{:S(2)}, u32[]{:S(2)}) collective-permute-start(bf16[2,16,1536]{2,1,0:T(8,128)(2,1)S(1)} %get-tuple-element.10), channel_id=1, source_target_pairs={{2,0},{4,2},{6,4},{8,6},{10,8},{12,10},{14,12},{16,14},{18,16},{20... | collective-permute-start | bytes 294920 | tf_op jit(solution)/shard_map/ppermute | solution.py:25
  19.1 101.7 %collective-permute-start = (bf16[2,16,1536]{2,1,0:T(8,128)(2,1)S(1)}, bf16[2,16,1536]{2,1,0:T(8,128)(2,1)S(1)}, u32[]{:S(2)}, u32[]{:S(2)}) collective-permute-start(bf16[2,16,1536]{2,1,0:T(8,128)(2,1)S(1)} %get-tuple-element.9), channel_id=1, source_target_pairs={{0,2},{2,4},{4,6},{6,8},{8,10},{10,12},{12,14},{14,16},{16,18},{18... | collective-permute-start | bytes 294920 | tf_op jit(solution)/shard_map/ppermute | solution.py:24
  21.1 467.6 %all-gather.13.cloned.1.call-start = ((), (), s32[]{:S(2)}) async-start(), calls=%async_computation.3 | async-start | bytes 1392640 | tf_op jit(solution)/shard_map/all_gather | solution.py:105
  120.8 98.8 %copy-start.20 = (bf16[2,32,1536]{2,1,0:T(8,128)(2,1)S(1)}, bf16[2,32,1536]{2,1,0:T(8,128)(2,1)}, u32[]{:S(2)}) copy-start(bf16[2,32,1536]{2,1,0:T(8,128)(2,1)} %param.11) | copy-start | bytes 589828
  122.4 204.9 %copy-start.17 = (f32[2,32,384]{2,1,0:T(8,128)}, f32[2,32,384]{2,1,0:T(8,128)S(1)}, u32[]{:S(2)}) copy-start(f32[2,32,384]{2,1,0:T(8,128)S(1)} %fusion.44) | copy-start | bytes 294916
  122.4 202.4 %copy-start.31 = (f32[1536]{0:T(1024)S(1)}, f32[1536]{0:T(1024)}, u32[]{:S(2)}) copy-start(f32[1536]{0:T(1024)} %param.15) | copy-start | bytes 18436
  221.2 106.1 %copy-start.37 = (f32[2,32]{1,0:T(2,128)}, f32[2,32]{1,0:T(2,128)S(1)}, u32[]{:S(2)}) copy-start(f32[2,32]{1,0:T(2,128)S(1)} %add_rsqrt_fusion) | copy-start | bytes 772
  324.9 3.2 copy-start.39
  327.3 133.1 %copy-start.19 = (bf16[2,32,896]{2,1,0:T(8,128)(2,1)}, bf16[2,32,896]{2,1,0:T(8,128)(2,1)S(1)}, u32[]{:S(2)}) copy-start(bf16[2,32,896]{2,1,0:T(8,128)(2,1)S(1)} %fusion.28) | copy-start | bytes 344068
  328.8 161.5 %copy-start.13 = (pred[4,32,512]{2,1,0:T(8,128)(4,1)}, pred[4,32,512]{2,1,0:T(8,128)(4,1)S(1)}, u32[]{:S(2)}) copy-start(pred[4,32,512]{2,1,0:T(8,128)(4,1)S(1)} %compare_and_fusion.1) | copy-start | bytes 196612
  329.5 118.3 %copy-start.11 = (bf16[2,32,640]{2,1,0:T(8,128)(2,1)S(1)}, bf16[2,32,640]{2,1,0:T(8,128)(2,1)}, u32[]{:S(2)}) copy-start(bf16[2,32,640]{2,1,0:T(8,128)(2,1)} %slice.121) | copy-start | bytes 245764
  428.3 19.4 %copy-start.25 = (bf16[32,4,96]{2,1,0:T(4,128)(2,1)}, bf16[32,4,96]{2,1,0:T(4,128)(2,1)S(1)}, u32[]{:S(2)}) copy-start(bf16[32,4,96]{2,1,0:T(4,128)(2,1)S(1)} %reshape.251) | copy-start | bytes 73732
  447.9 30.5 %collective-permute-start.2 = (bf16[2,32,640]{2,1,0:T(8,128)(2,1)S(1)}, bf16[2,32,640]{2,1,0:T(8,128)(2,1)S(1)}, u32[]{:S(2)}, u32[]{:S(2)}) collective-permute-start(bf16[2,32,640]{2,1,0:T(8,128)(2,1)S(1)} %copy-done.11), channel_id=1, source_target_pairs={{0,2},{2,4},{4,6},{6,8},{8,10},{10,12},{12,14},{14,16},{16,18},{18... | collective-permute-start | bytes 245768 | tf_op jit(solution)/shard_map/ppermute | solution.py:24
  450.6 27.8 %collective-permute-start.3 = (bf16[2,32,640]{2,1,0:T(8,128)(2,1)S(1)}, bf16[2,32,640]{2,1,0:T(8,128)(2,1)S(1)}, u32[]{:S(2)}, u32[]{:S(2)}) collective-permute-start(bf16[2,32,640]{2,1,0:T(8,128)(2,1)S(1)} %copy-done.11), channel_id=1, source_target_pairs={{2,0},{4,2},{6,4},{8,6},{10,8},{12,10},{14,12},{16,14},{18,16},{20... | collective-permute-start | bytes 245768 | tf_op jit(solution)/shard_map/ppermute | solution.py:25
  460.5 17.2 %slice-start.2 = ((bf16[2,32,896]{2,1,0:T(8,128)(2,1)}), bf16[2,32,384]{2,1,0:T(8,128)(2,1)S(1)}, s32[]{:S(2)}) async-start(bf16[2,32,896]{2,1,0:T(8,128)(2,1)} %copy-done.19), calls=%async_computation.7 | async-start | bytes 98304 | tf_op jit(solution)/shard_map/slice | solution.py:179
  460.6 29.4 %copy-start.15 = (bf16[2,32,4,64]{3,2,1,0:T(4,128)(2,1)}, bf16[2,32,4,64]{3,2,1,0:T(4,128)(2,1)S(1)}, u32[]{:S(2)}) copy-start(bf16[2,32,4,64]{3,2,1,0:T(4,128)(2,1)S(1)} %reshape.248) | copy-start | bytes 98308
  476.9 57.9 %copy-start.2 = (bf16[2,512,256]{1,2,0:T(8,128)(2,1)}, bf16[2,512,256]{1,2,0:T(8,128)(2,1)S(1)}, u32[]{:S(2)}) copy-start(bf16[2,512,256]{1,2,0:T(8,128)(2,1)S(1)} %copy.129) | copy-start | bytes 1572868
  478.5 11.4 %copy-start.12 = (bf16[2,96,256]{1,2,0:T(8,128)(2,1)}, bf16[2,96,256]{1,2,0:T(8,128)(2,1)S(1)}, u32[]{:S(2)}) copy-start(bf16[2,96,256]{1,2,0:T(8,128)(2,1)S(1)} %copy.113) | copy-start | bytes 294916
  489.9 2.0 copy-start.6
  492.2 2.1 copy-start.22
  492.2 2.1 copy-start.29
  492.2 3.0 copy-start.7
  492.3 3.0 copy-start.14
  493.0 2.2 copy-start.33
  498.2 21.6 %copy-start.30 = (bf16[2,4,32,96]{3,2,1,0:T(8,128)(2,1)}, bf16[2,4,32,96]{3,2,1,0:T(8,128)(2,1)S(1)}, u32[]{:S(2)}) copy-start(bf16[2,4,32,96]{3,2,1,0:T(8,128)(2,1)S(1)} %fusion.45) | copy-start | bytes 147460
  520.5 14.3 %copy-start.27 = (pred[4,512,32]{1,2,0:T(8,128)(4,1)S(1)}, pred[4,512,32]{1,2,0:T(8,128)(4,1)}, u32[]{:S(2)}) copy-start(pred[4,512,32]{1,2,0:T(8,128)(4,1)} %compare_and_fusion) | copy-start | bytes 196612
  520.5 14.3 %copy-start.28 = (bf16[2,32,4,64]{3,2,1,0:T(4,128)(2,1)S(1)}, bf16[2,32,4,64]{3,2,1,0:T(4,128)(2,1)}, u32[]{:S(2)}) copy-start(bf16[2,32,4,64]{3,2,1,0:T(4,128)(2,1)} %reshape.257) | copy-start | bytes 98308
  521.0 14.9 %copy-start.4 = (f32[2,96,384]{2,1,0:T(8,128)}, f32[2,96,384]{2,1,0:T(8,128)S(1)}, u32[]{:S(2)}) copy-start(f32[2,96,384]{2,1,0:T(8,128)S(1)} %reshape.255) | copy-start | bytes 884740
  521.7 15.1 %copy-start.35 = (f32[2,4,512]{2,1,0:T(4,128)S(1)}, f32[2,4,512]{2,1,0:T(4,128)}, u32[]{:S(2)}) copy-start(f32[2,4,512]{2,1,0:T(4,128)} %copy.135) | copy-start | bytes 49156
  521.7 25.5 %collective-permute-start.4 = (bf16[2,32,640]{2,1,0:T(8,128)(2,1)}, bf16[2,32,640]{2,1,0:T(8,128)(2,1)}, u32[]{:S(2)}, u32[]{:S(2)}) collective-permute-start(bf16[2,32,640]{2,1,0:T(8,128)(2,1)} %get-tuple-element.7), channel_id=1, source_target_pairs={{0,2},{2,4},{4,6},{6,8},{8,10},{10,12},{12,14},{14,16},{16,18},{18... | collective-permute-start | bytes 245768 | tf_op jit(solution)/shard_map/ppermute | solution.py:33
  523.8 23.5 %collective-permute-start.5 = (bf16[2,32,640]{2,1,0:T(8,128)(2,1)}, bf16[2,32,640]{2,1,0:T(8,128)(2,1)}, u32[]{:S(2)}, u32[]{:S(2)}) collective-permute-start(bf16[2,32,640]{2,1,0:T(8,128)(2,1)} %get-tuple-element.8), channel_id=1, source_target_pairs={{2,0},{4,2},{6,4},{8,6},{10,8},{12,10},{14,12},{16,14},{18,16},{20... | collective-permute-start | bytes 245768 | tf_op jit(solution)/shard_map/ppermute | solution.py:33
  536.8 11.6 %copy-start = (bf16[1536,896]{1,0:T(8,128)(2,1)S(1)}, bf16[1536,896]{1,0:T(8,128)(2,1)}, u32[]{:S(2)}) copy-start(bf16[1536,896]{1,0:T(8,128)(2,1)} %all-gather.11.cloned.1.call-done) | copy-start | bytes 8257540
  539.3 8.0 %copy-start.5 = (f32[2,96,384]{2,1,0:T(8,128)S(1)}, f32[2,96,384]{2,1,0:T(8,128)}, u32[]{:S(2)}) copy-start(f32[2,96,384]{2,1,0:T(8,128)} %copy-done.4) | copy-start | bytes 884740
  539.3 9.1 %copy-start.32 = (f32[1536]{0:T(1024)S(1)}, f32[1536]{0:T(1024)}, u32[]{:S(2)}) copy-start(f32[1536]{0:T(1024)} %param.15) | copy-start | bytes 18436
  547.3 3.1 copy-start.18
  547.3 3.1 copy-start.23
  547.3 3.1 copy-start.38
  548.4 2.0 copy-start.1
  548.4 11.5 %copy-start.3 = (bf16[3,1536,384]{2,1,0:T(8,128)(2,1)S(1)}, bf16[3,1536,384]{2,1,0:T(8,128)(2,1)}, u32[]{:S(2)}) copy-start(bf16[3,1536,384]{2,1,0:T(8,128)(2,1)} %all-gather.7.cloned.1.call-done) | copy-start | bytes 10616836
  551.0 9.4 %collective-permute-start.7 = (bf16[2,16,384]{2,1,0:T(8,128)(2,1)S(1)}, bf16[2,16,384]{2,1,0:T(8,128)(2,1)S(1)}, u32[]{:S(2)}, u32[]{:S(2)}) collective-permute-start(bf16[2,16,384]{2,1,0:T(8,128)(2,1)S(1)} %get-tuple-element.14), channel_id=1, source_target_pairs={{0,2},{2,4},{4,6},{6,8},{8,10},{10,12},{12,14},{14,16},{16,18},{18... | collective-permute-start | bytes 73736 | tf_op jit(solution)/shard_map/ppermute | solution.py:24
  552.9 8.0 %collective-permute-start.6 = (bf16[2,16,384]{2,1,0:T(8,128)(2,1)S(1)}, bf16[2,16,384]{2,1,0:T(8,128)(2,1)S(1)}, u32[]{:S(2)}, u32[]{:S(2)}) collective-permute-start(bf16[2,16,384]{2,1,0:T(8,128)(2,1)S(1)} %get-tuple-element.13), channel_id=1, source_target_pairs={{2,0},{4,2},{6,4},{8,6},{10,8},{12,10},{14,12},{16,14},{18,16},{20... | collective-permute-start | bytes 73736 | tf_op jit(solution)/shard_map/ppermute | solution.py:25
  (9 other events, 11.8 us)
Sparse Core Ops, SparseCore 0:
  9.4 108.0 all-gather.6
  119.6 99.8 all-gather.8
  221.6 103.1 all-gather.10
  326.8 99.6 all-gather.14
  429.3 59.3 all-gather.12
